TPU v7x, 32 devices: a whole 2x2x4 slice. The times are simulated.
32 devices in a mesh: query: 8 (over z, y), tensor: 2 (over x), dp: 2 (over core).
Axes of the slice: x: 2, y: 2, z: 4, core: 2. Of those that a mesh axis runs over, the one named last changes fastest.
Arguments:
- hidden: bfloat16 [16, 1024, 14336], P(('query', 'dp'), None, 'tensor'), may hold values from -6 to 6
- out_grad: bfloat16 [16, 1024, 4096], P(('query', 'dp'), None, 'tensor'), may hold values from -6 to 6
- proj_in: bfloat16 [14336, 64], P('tensor'), may hold values from -0.046875 to 0.046875
- proj_out: bfloat16 [4096, 64], P('tensor'), may hold values from -0.09375 to 0.09375
- seg_ids: int32 [16, 1024], P(('query', 'dp')), may hold values from 0 to 31, never falling along the last dimension, each value on 1 to 288 neighbouring positions
- queries: bfloat16 [1024, 4096], P(('query', 'dp'), 'tensor'), may hold values from -0.01171875 to 0.01171875
Outputs:
- scores: float32 [512, 1024], P('tensor', ('query', 'dp'))
All inputs are finite; a program needn't handle non-finite values.
Results may differ from a plain program's by a relative error of at most 0.004.
Values may be sent and summed in bfloat16 or wider, within the bound.
No kernel may reach another device: no remote copies, remote signals or barrier semaphores. Data moves between devices by JAX's collectives and lax.ppermute only.
A program may use at most 64 MiB of HBM per device.

v0:
```python
import jax
import jax.numpy as jnp
from jax import lax
from jax.sharding import PartitionSpec as P

SEGS = 32


def local(hidden, out_grad, proj_in, proj_out, seg_ids, queries):
    tokens = hidden[0]
    grads = out_grad[0]
    segment = seg_ids[0]
    part_in = jnp.dot(tokens, proj_in, preferred_element_type=jnp.float32)
    part_out = jnp.dot(grads, proj_out, preferred_element_type=jnp.float32)
    act_proj = lax.psum(part_in, "tensor")
    grad_share = lax.psum_scatter(part_out, "tensor", scatter_dimension=1, tiled=True)
    outer = (
        (grad_share[:, :, None] * act_proj[:, None, :])
        .reshape(tokens.shape[0], -1)
        .astype(jnp.bfloat16)
    )
    member = (segment[None, :] == jnp.arange(SEGS, dtype=jnp.int32)[:, None]).astype(jnp.bfloat16)
    doc_feats = jnp.dot(member, outer, preferred_element_type=jnp.float32).astype(jnp.bfloat16)
    table = lax.dot_general(
        lax.all_gather(doc_feats, ("query", "dp"), axis=0, tiled=True),
        queries,
        (((1,), (1,)), ((), ())),
        preferred_element_type=jnp.float32,
    )
    return lax.psum_scatter(table, "tensor", scatter_dimension=0, tiled=True)


def solution(mesh):
    in_specs = (
        P(("query", "dp"), None, "tensor"),
        P(("query", "dp"), None, "tensor"),
        P("tensor", None),
        P("tensor", None),
        P(("query", "dp"), None),
        P(("query", "dp"), "tensor"),
    )
    out_specs = P("tensor", ("query", "dp"))
    return jax.shard_map(local, mesh=mesh, in_specs=in_specs, out_specs=out_specs, check_vma=False)
```

profile of v0, /device:TPU:0, one launch (start us, length us, event | category | flops | bytes accessed | tf_op | source)
XLA Modules:
  0.0 123.0 jit_solution(5992180469758918118)
XLA Ops:
  6.5 0.0 copy-start
  6.5 0.0 all-reduce.2.cloned.1.call-start
  6.5 1.2 copy-done
  7.7 10.4 %fusion = f32[1024,64]{0,1:T(8,128)} fusion(bf16[7168,64]{0,1:T(8,128)(2,1)S(1)} %copy-done, bf16[1,1024,7168]{2,1,0:T(8,128)(2,1)} %param.6), kind=kOutput, calls=%fused_computation | convolution fusion | flops 939524096 | bytes 15859712 | tf_op jit(solution)/shard_map/dot_general | solution.py:13
  18.1 0.0 all-reduce.2.cloned.1.call-update
  18.2 0.0 copy-start.3
  18.2 0.0 reduce-scatter.3.cloned.1.call-start
  18.2 0.0 copy-done.1
  18.2 4.3 %fusion.2 = f32[1024,64]{0,1:T(8,128)} fusion(bf16[2048,64]{0,1:T(8,128)(2,1)S(1)} %copy-done.1, bf16[1,1024,2048]{2,1,0:T(8,128)(2,1)} %param.7), kind=kOutput, calls=%fused_computation.3 | convolution fusion | flops 268435456 | bytes 4718592 | tf_op jit(solution)/shard_map/dot_general | solution.py:14
  22.5 0.0 reduce-scatter.3.cloned.1.call-update
  22.5 0.0 copy-start.2
  22.6 0.0 all-gather.2.cloned.1.call-start
  22.6 21.7 %all-reduce.2.cloned.1.call-done = f32[1024,64]{0,1:T(8,128)} async-done(((f32[1024,64]{0,1:T(8,128)}), f32[1024,64]{0,1:T(8,128)}) %all-reduce.2.cloned.1.call-update) | async-done | bytes 262160 | tf_op jit(solution)/shard_map/psum | solution.py:15
  44.3 14.0 %reduce-scatter.3.cloned.1.call-done = f32[1024,32]{0,1:T(8,128)} async-done(((f32[1024,64]{0,1:T(8,128)}), f32[1024,32]{0,1:T(8,128)}) %reduce-scatter.3.cloned.1.call-update) | async-done | bytes 131088 | tf_op jit(solution)/shard_map/reduce_scatter | solution.py:16
  58.4 2.2 %multiply_convert_fusion = bf16[1024,32,64]{0,2,1:T(8,128)(2,1)S(1)} fusion(f32[1024,64]{0,1:T(8,128)} %all-reduce.2.cloned.1.call-done, f32[1024,32]{0,1:T(8,128)} %reduce-scatter.3.cloned.1.call-done), kind=kLoop, calls=%fused_computation.2 | loop fusion | flops 4194304 | bytes 4587520 | tf_op jit(solution)/shard_map/convert_element_type | solution.py:20
  60.6 0.0 copy-done.3
  60.6 2.0 %convolution_convert_fusion = bf16[32,2048]{1,0:T(8,128)(2,1)} fusion(bf16[1024,2048]{0,1:T(8,128)(2,1)S(1)} %bitcast.13, s32[1024]{0:T(1024)S(1)} %bitcast.14), kind=kOutput, calls=%fused_computation.5 | convolution fusion | flops 134316032 | bytes 4329472 | tf_op jit(solution)/shard_map/dot_general | solution.py:23
  62.6 0.0 all-gather.2.cloned.1.call-update
  62.6 0.0 reduce-scatter.5.cloned.1.call-start
  62.7 41.6 %all-gather.2.cloned.1.call-done = bf16[512,2048]{1,0:T(8,128)(2,1)} async-done(((bf16[32,2048]{1,0:T(8,128)(2,1)}), bf16[512,2048]{1,0:T(8,128)(2,1)}) %all-gather.2.cloned.1.call-update) | async-done | bytes 2097168 | tf_op jit(solution)/shard_map/all_gather | solution.py:25
  104.2 0.0 copy-done.2
  104.2 3.0 %fusion.5 = f32[512,64]{0,1:T(8,128)} fusion(bf16[512,2048]{1,0:T(8,128)(2,1)} %all-gather.2.cloned.1.call-done, bf16[64,2048]{1,0:T(8,128)(2,1)S(1)} %copy-done.2), kind=kOutput, calls=%fused_computation.8 | convolution fusion | flops 134217728 | bytes 2490368 | tf_op jit(solution)/shard_map/dot_general | solution.py:24
  107.2 0.0 reduce-scatter.5.cloned.1.call-update
  107.3 9.2 %reduce-scatter.5.cloned.1.call-done = f32[256,64]{0,1:T(8,128)} async-done(((f32[512,64]{0,1:T(8,128)}), f32[256,64]{0,1:T(8,128)}) %reduce-scatter.5.cloned.1.call-update) | async-done | bytes 65552 | tf_op jit(solution)/shard_map/reduce_scatter | solution.py:30
  (1 shorter events, 0.0 us)
Async XLA Ops:
  6.5 1.2 copy-start
  6.5 11.7 %copy-start.1 = (bf16[2048,64]{0,1:T(8,128)(2,1)S(1)}, bf16[2048,64]{0,1:T(8,128)(2,1)}, u32[]{:S(2)}) copy-start(bf16[2048,64]{0,1:T(8,128)(2,1)} %param.9) | copy-start | bytes 786436
  6.5 37.8 %all-reduce.2.cloned.1.call-start = ((), (), s32[]{:S(2)}) async-start(), calls=%async_computation.3 | async-start | bytes 524288 | tf_op jit(solution)/shard_map/psum | solution.py:15
  18.2 42.5 %copy-start.3 = (s32[1,1024]{1,0:T(1,128)S(1)}, s32[1,1024]{1,0:T(1,128)}, u32[]{:S(2)}) copy-start(s32[1,1024]{1,0:T(1,128)} %param.10) | copy-start | bytes 12292
  18.2 40.2 %reduce-scatter.3.cloned.1.call-start = ((), (), s32[]{:S(2)}) async-start(), calls=%async_computation.2 | async-start | bytes 393216 | tf_op jit(solution)/shard_map/reduce_scatter | solution.py:16
  22.5 81.7 %copy-start.2 = (bf16[64,2048]{1,0:T(8,128)(2,1)S(1)}, bf16[64,2048]{1,0:T(8,128)(2,1)}, u32[]{:S(2)}) copy-start(bf16[64,2048]{1,0:T(8,128)(2,1)} %param.11) | copy-start | bytes 786436
  22.6 81.7 %all-gather.2.cloned.1.call-start = ((), (), s32[]{:S(2)}) async-start(), calls=%async_computation.4 | async-start | bytes 2228224 | tf_op jit(solution)/shard_map/all_gather | solution.py:25
  62.6 53.9 %reduce-scatter.5.cloned.1.call-start = ((), (), s32[]{:S(2)}) async-start(), calls=%async_computation.5 | async-start | bytes 196608 | tf_op jit(solution)/shard_map/reduce_scatter | solution.py:30
Sparse Core Ops, SparseCore 0:
  18.3 26.0 all-reduce.1
  46.6 11.7 reduce-scatter.2
  62.7 41.4 all-gather.1
  107.4 9.0 reduce-scatter.4
where the time goes:
time: 123 us
  waiting for transfers between devices  86.6 us (70%)
  matrix products  19.7 us (16%)
  between operations  13.2 us (11%)
  other arithmetic  2.24 us (2%)
    all_gather x1, waiting for transfers between devices, local(): lax.all_gather(doc_feats, ('query', 'dp'), axis=0, tiled=True)  41.6 us
    psum x1, waiting for transfers between devices, local(): act_proj = lax.psum(part_in, 'tensor')  21.7 us
    reduce_scatter x1, waiting for transfers between devices, local(): lax.psum_scatter(part_out, 'tensor', scatter_dimension=1, tiled=True)  14 us
    dot_general x1, matrix products, local(): part_in = jnp.dot(tokens, proj_in, preferred_element_type=jnp.float32)  10.4 us
    reduce_scatter x1, waiting for transfers between devices, local(): return lax.psum_scatter(table, 'tensor', scatter_dimension=0, tiled=True)  9.23 us
    dot_general x1, matrix products, local(): part_out = jnp.dot(grads, proj_out, preferred_element_type=jnp.float32)  4.28 us
    dot_general x1, matrix products, local(): lax.dot_general(lax.all_gather(doc_feats, ('query', 'dp'), axis=0, tiled=...  3 us
  transfers between devices with their start and end apart: 4, of which 4 were waited for; matrix products, arithmetic and copies ran while one was open for 3% of the time, Pallas kernels for 0%

commit v1 on v0

--- a/solution.py
+++ b/solution.py
@@ -12,7 +12,7 @@
     segment = seg_ids[0]
     part_in = jnp.dot(tokens, proj_in, preferred_element_type=jnp.float32)
     part_out = jnp.dot(grads, proj_out, preferred_element_type=jnp.float32)
-    act_proj = lax.psum(part_in, "tensor")
+    act_proj = jnp.sum(lax.all_gather(part_in, "tensor"), axis=0)
     grad_share = lax.psum_scatter(part_out, "tensor", scatter_dimension=1, tiled=True)
     outer = (
         (grad_share[:, :, None] * act_proj[:, None, :])

time: 123 us -> 98.2 us (0.80)
  waiting for transfers between devices: 86.6 us -> 52.4 us
  blocking collectives: 0 us -> 10.1 us
    psum x1 -> x0, waiting for transfers between devices: 21.7 us -> none  [local(): act_proj = lax.psum(part_in, 'tensor')]
    reduce_scatter x1, waiting for transfers between devices: 14 us -> 0.02 us  [local(): lax.psum_scatter(part_out, 'tensor', scatter_dimension=1, tiled=True)]
    all_gather x0 -> x1, blocking collectives: none -> 10.1 us  [local(): act_proj = jnp.sum(lax.all_gather(part_in, 'tensor'), axis=0)]
    all_gather x1, waiting for transfers between devices: 41.6 us -> 43.1 us  [local(): lax.all_gather(doc_feats, ('query', 'dp'), axis=0, tiled=True)]
  transfers between devices with their start and end apart: 4 -> 3, of which waited for: 4 -> 2; matrix products, arithmetic and copies ran while one was open for 3% -> 11% of each run, Pallas kernels for 0% -> 0%
where the time goes in v1:
time: 98.2 us; the launch traced here: 98 us
  waiting for transfers between devices  52.4 us (53%)
  matrix products  19.1 us (19%)
  between operations  13.2 us (13%)
  blocking collectives  10.1 us (10%)
  other arithmetic  2.81 us (3%)
    all_gather x1, waiting for transfers between devices, local(): lax.all_gather(doc_feats, ('query', 'dp'), axis=0, tiled=True)  43.1 us
    all_gather x1, blocking collectives, local(): act_proj = jnp.sum(lax.all_gather(part_in, 'tensor'), axis=0)  10.1 us
    dot_general x1, matrix products, local(): part_in = jnp.dot(tokens, proj_in, preferred_element_type=jnp.float32)  9.73 us
    reduce_scatter x1, waiting for transfers between devices, local(): return lax.psum_scatter(table, 'tensor', scatter_dimension=0, tiled=True)  9.23 us
    dot_general x1, matrix products, local(): part_out = jnp.dot(grads, proj_out, preferred_element_type=jnp.float32)  4.38 us
    dot_general x1, matrix products, local(): lax.dot_general(lax.all_gather(doc_feats, ('query', 'dp'), axis=0, tiled=...  3 us
    convert_element_type x1, other arithmetic, local(): outer = (grad_share[:, :, None] * act_proj[:, None, :]).reshape(tokens.sh...  2.19 us
    dot_general x1, matrix products, local(): jnp.dot(member, outer, preferred_element_type=jnp.float32)  1.97 us
  transfers between devices with their start and end apart: 3, of which 2 were waited for; matrix products, arithmetic and copies ran while one was open for 11% of the time, Pallas kernels for 0%

profile of v1, /device:TPU:0, one launch (start us, length us, event | category | flops | bytes accessed | tf_op | source)
XLA Modules:
  0.0 98.0 jit_solution(13894252885614121842)
XLA Ops:
  6.5 0.0 copy-start
  6.5 0.0 reduce-scatter.3.cloned.1.call-start
  6.5 4.4 %fusion.2 = f32[1024,64]{0,1:T(8,128)} fusion(bf16[2048,64]{0,1:T(8,128)(2,1)} %param.9, bf16[1,1024,2048]{2,1,0:T(8,128)(2,1)} %param.7), kind=kOutput, calls=%fused_computation.3 | convolution fusion | flops 268435456 | bytes 4718592 | tf_op jit(solution)/shard_map/dot_general | solution.py:14
  10.9 0.0 reduce-scatter.3.cloned.1.call-update
  10.9 0.0 all-gather.3.cloned.1.call-start
  11.0 0.0 copy-done
  11.0 9.7 %fusion = f32[1024,64]{0,1:T(8,128)S(1)} fusion(bf16[7168,64]{0,1:T(8,128)(2,1)S(1)} %copy-done, bf16[1,1024,7168]{2,1,0:T(8,128)(2,1)} %param.6), kind=kOutput, calls=%fused_computation | convolution fusion | flops 939524096 | bytes 15859712 | tf_op jit(solution)/shard_map/dot_general | solution.py:13
  20.7 0.0 copy-start.2
  20.7 10.1 %all-gather = f32[2048,64]{0,1:T(8,128)S(1)} all-gather(f32[1024,64]{0,1:T(8,128)S(1)} %fusion), channel_id=2, replica_groups=mesh['query'=8,'tensor'=2,'dp'=2] {'tensor'}, dimensions={0}, use_global_device_ids=true | all-gather | bytes 786432 | tf_op jit(solution)/shard_map/all_gather | solution.py:15
  30.8 0.4 reshape.7
  31.2 0.6 reduce_sum.9
  31.9 0.0 copy-start.1
  31.9 0.0 reduce-scatter.3.cloned.1.call-done
  31.9 2.2 %multiply_convert_fusion = bf16[1024,32,64]{0,2,1:T(8,128)(2,1)S(1)} fusion(f32[1024,64]{0,1:T(8,128)S(1)} %reduce_sum.9, f32[1024,32]{0,1:T(8,128)} %reduce-scatter.3.cloned.1.call-done), kind=kLoop, calls=%fused_computation.2 | loop fusion | flops 4194304 | bytes 4587520 | tf_op jit(solution)/shard_map/convert_element_type | solution.py:20
  34.1 0.0 copy-done.2
  34.1 2.0 %convolution_convert_fusion = bf16[32,2048]{1,0:T(8,128)(2,1)} fusion(bf16[1024,2048]{0,1:T(8,128)(2,1)S(1)} %bitcast.15, s32[1024]{0:T(1024)S(1)} %bitcast.16), kind=kOutput, calls=%fused_computation.5 | convolution fusion | flops 134316032 | bytes 4329472 | tf_op jit(solution)/shard_map/dot_general | solution.py:23
  36.1 0.0 all-gather.3.cloned.1.call-update
  36.1 0.0 reduce-scatter.5.cloned.1.call-start
  36.2 43.1 %all-gather.3.cloned.1.call-done = bf16[512,2048]{1,0:T(8,128)(2,1)} async-done(((bf16[32,2048]{1,0:T(8,128)(2,1)}), bf16[512,2048]{1,0:T(8,128)(2,1)}) %all-gather.3.cloned.1.call-update) | async-done | bytes 2097168 | tf_op jit(solution)/shard_map/all_gather | solution.py:25
  79.2 0.0 copy-done.1
  79.2 3.0 %fusion.5 = f32[512,64]{0,1:T(8,128)} fusion(bf16[512,2048]{1,0:T(8,128)(2,1)} %all-gather.3.cloned.1.call-done, bf16[64,2048]{1,0:T(8,128)(2,1)S(1)} %copy-done.1), kind=kOutput, calls=%fused_computation.8 | convolution fusion | flops 134217728 | bytes 2490368 | tf_op jit(solution)/shard_map/dot_general | solution.py:24
  82.2 0.0 reduce-scatter.5.cloned.1.call-update
  82.3 9.2 %reduce-scatter.5.cloned.1.call-done = f32[256,64]{0,1:T(8,128)} async-done(((f32[512,64]{0,1:T(8,128)}), f32[256,64]{0,1:T(8,128)}) %reduce-scatter.5.cloned.1.call-update) | async-done | bytes 65552 | tf_op jit(solution)/shard_map/reduce_scatter | solution.py:30
Async XLA Ops:
  6.5 4.5 %copy-start = (bf16[7168,64]{0,1:T(8,128)(2,1)S(1)}, bf16[7168,64]{0,1:T(8,128)(2,1)}, u32[]{:S(2)}) copy-start(bf16[7168,64]{0,1:T(8,128)(2,1)} %param.8) | copy-start | bytes 2752516
  6.5 25.4 %reduce-scatter.3.cloned.1.call-start = ((), (), s32[]{:S(2)}) async-start(), calls=%async_computation.2 | async-start | bytes 393216 | tf_op jit(solution)/shard_map/reduce_scatter | solution.py:16
  10.9 68.3 %all-gather.3.cloned.1.call-start = ((), (), s32[]{:S(2)}) async-start(), calls=%async_computation.3 | async-start | bytes 2228224 | tf_op jit(solution)/shard_map/all_gather | solution.py:25
  20.7 13.4 %copy-start.2 = (s32[1,1024]{1,0:T(1,128)S(1)}, s32[1,1024]{1,0:T(1,128)}, u32[]{:S(2)}) copy-start(s32[1,1024]{1,0:T(1,128)} %param.10) | copy-start | bytes 12292
  31.9 47.4 %copy-start.1 = (bf16[64,2048]{1,0:T(8,128)(2,1)S(1)}, bf16[64,2048]{1,0:T(8,128)(2,1)}, u32[]{:S(2)}) copy-start(bf16[64,2048]{1,0:T(8,128)(2,1)} %param.11) | copy-start | bytes 786436
  36.1 55.4 %reduce-scatter.5.cloned.1.call-start = ((), (), s32[]{:S(2)}) async-start(), calls=%async_computation.4 | async-start | bytes 196608 | tf_op jit(solution)/shard_map/reduce_scatter | solution.py:30
Sparse Core Ops, SparseCore 0:
  11.1 14.4 reduce-scatter.2
  36.2 42.9 all-gather.2
  82.4 9.0 reduce-scatter.4
